TPU v7x, 32 devices: a whole 2x2x4 slice. The times are simulated.
32 devices in a mesh: groups: 2 (over x), tm: 8 (over z, y), space: 2 (over core).
Axes of the slice: x: 2, y: 2, z: 4, core: 2. Of those that a mesh axis runs over, the one named last changes fastest.
Arguments:
- latents: bfloat16 [32, 12, 80, 2240], P(('groups', 'tm'), 'space'), parts along dimension 0, may hold values from -8 to 8
- proj_weight: bfloat16 [2240, 3360], P('tm'), may hold values from -0.125 to 0.125
Outputs:
- attended: bfloat16 [32, 12, 80, 1120], P(('groups', 'tm'), 'space'), parts along dimension 0
There are 2 independent parts, one for each index of `groups`. A program takes and returns all parts, laid end to end along the dimension named above; an argument that names none is the same for every part. Nothing has to cross between parts.
All inputs are finite; a program needn't handle non-finite values.
Results may differ from a plain program's by a relative error of at most 0.0034.
Values may be sent and summed in bfloat16 or wider, within the bound.
A program may use at most 128 MiB of HBM per device.

v0:
```python
import jax
import jax.numpy as jnp
from jax import lax
from jax.sharding import PartitionSpec as P

HEADS = 10
HEAD = 112


def entering(value, axis, join, neutral):
    count, mine = (lax.axis_size(axis), lax.axis_index(axis))
    pieces = jax.tree.map(lambda part: lax.all_gather(part, axis), value)
    subtotal = jax.tree.map(
        lambda part, zero: jnp.full_like(part, 0) + jnp.asarray(zero, part.dtype), value, neutral
    )

    def hop(position, subtotal):
        longer = join(subtotal, jax.tree.map(lambda part: part[position], pieces))
        return jax.tree.map(lambda new, old: jnp.where(position < mine, new, old), longer, subtotal)

    return lax.fori_loop(0, count - 1, hop, subtotal)


def add_pairs(earlier, later):
    return (earlier[0] + later[0], earlier[1] + later[1])


def make_adder(flat, shard_rows):
    return jnp.dot(flat, shard_rows, preferred_element_type=jnp.float32)


def project_rows(flat, columns):
    return make_adder(flat, lax.all_gather(columns, "tm", axis=0, tiled=True))


def local_states(projected, heads_here):
    count = projected.shape[0]
    split = projected.astype(jnp.bfloat16).reshape(count, 3, heads_here, HEAD)
    queries = jax.nn.relu(split[:, 0])
    key_feats = jax.nn.relu(split[:, 1])
    values = split[:, 2]
    states = jnp.einsum("nhe,nhf->hef", key_feats, values, preferred_element_type=jnp.float32)
    key_sums = jnp.sum(key_feats, axis=0, dtype=jnp.float32)
    return (queries, states, key_sums)


def apply_states(queries, states, key_sums):
    numerator = jnp.einsum(
        "nhe,hef->nhf", queries, states.astype(jnp.bfloat16), preferred_element_type=jnp.float32
    )
    denominator = jnp.einsum(
        "nhe,he->nh", queries.astype(jnp.float32), key_sums, precision=lax.Precision.HIGHEST
    )
    return (numerator / (denominator[:, :, None] + 1.0)).astype(jnp.bfloat16)


def on_device(latents, proj_weight):
    frame_count, band_rows, column_count, channels = latents.shape
    shard_depth = proj_weight.shape[0]
    band_count = lax.axis_size("space")
    band_index = lax.axis_index("space")
    heads_here = HEADS // band_count
    grouped = proj_weight.reshape(shard_depth, 3, band_count, heads_here * HEAD)
    own_columns = lax.dynamic_index_in_dim(grouped, band_index, 2, keepdims=False)
    own_columns = own_columns.reshape(shard_depth, 3 * heads_here * HEAD)
    both_bands = lax.all_gather(latents, "space", axis=1, tiled=True)
    joined_rows = both_bands.shape[1]
    count = frame_count * joined_rows * column_count
    flat = both_bands.reshape(count, channels)
    projected = project_rows(flat, own_columns)
    queries, states, key_sums = local_states(projected, heads_here)
    identity = (jnp.zeros_like(states), jnp.zeros_like(key_sums))
    earlier = entering((states, key_sums), "tm", add_pairs, identity)
    attended = apply_states(queries, states + earlier[0], key_sums + earlier[1])
    attended = attended.reshape(frame_count, joined_rows, column_count, heads_here * HEAD)
    return lax.all_to_all(attended, "space", split_axis=1, concat_axis=3, tiled=True)


def solution(mesh):
    return jax.shard_map(
        on_device,
        mesh=mesh,
        in_specs=(P(("groups", "tm"), "space", None, None), P("tm", None)),
        out_specs=P(("groups", "tm"), "space", None, None),
        check_vma=False,
    )
```

profile of v0, /device:TPU:25, one launch (start us, length us, event | category | flops | bytes accessed | tf_op | source)
XLA Modules:
  0.0 272.0 jit_solution(16868224540163675632)
XLA Ops:
  6.5 0.0 all-gather.9.cloned.1.call-start
  6.5 0.7 all-gather.9.cloned.1.call-update
  7.3 0.0 all-gather.7.cloned.1.call-start
  7.3 5.4 %reshape.22 = bf16[280,3,2,560]{3,2,1,0:T(2,128)(2,1)S(1)} reshape(bf16[280,3360]{1,0:T(8,128)(2,1)} %param.5) | data formatting | bytes 3763200 | tf_op jit(solution)/shard_map/reshape | solution.py:63
  12.7 3.6 %constant_dynamic-slice_fusion = bf16[280,3,1,560]{3,2,1,0:T(2,128)(2,1)} fusion(bf16[280,3,2,560]{3,2,1,0:T(2,128)(2,1)S(1)} %reshape.22, s32[]{:T(128)S(6)} %select_n.42), kind=kLoop, calls=%fused_computation.21 | loop fusion | bytes 1881604 | tf_op jit(solution)/shard_map/jit(dynamic_index_in_dim)/dynamic_slice | solution.py:64
  16.3 6.2 %copy.25 = bf16[280,3,1,560]{0,3,1,2:T(8,128)(2,1)S(1)} copy(bf16[280,3,1,560]{3,2,1,0:T(2,128)(2,1)} %constant_dynamic-slice_fusion) | data formatting | bytes 1881600
  22.5 2.3 copy.13
  24.8 0.0 all-gather.7.cloned.1.call-update
  24.8 0.0 all-gather.11.cloned.1.call-start
  24.9 5.1 %all-gather.9.cloned.1.call-done = bf16[2,12,80,2240]{3,2,1,0:T(8,128)(2,1)} async-done(((bf16[2,6,80,2240]{3,2,1,0:T(8,128)(2,1)}), bf16[2,12,80,2240]{3,2,1,0:T(8,128)(2,1)}) %all-gather.9.cloned.1.call-update) | async-done | bytes 8601616 | tf_op jit(solution)/shard_map/all_gather | solution.py:66
  30.0 120.8 %all-gather.7.cloned.1.call-done = bf16[2240,1680]{1,0:T(8,128)(2,1)} async-done(((bf16[280,1680]{1,0:T(8,128)(2,1)}), bf16[2240,1680]{1,0:T(8,128)(2,1)}) %all-gather.7.cloned.1.call-update) | async-done | bytes 7526416 | tf_op jit(solution)/shard_map/all_gather | solution.py:33
  150.8 22.4 %convolution_convert_fusion = bf16[1680,1920]{1,0:T(8,128)(2,1)S(1)} fusion(bf16[2240,1680]{1,0:T(8,128)(2,1)} %all-gather.7.cloned.1.call-done, bf16[1920,2240]{1,0:T(8,128)(2,1)} %bitcast.54), kind=kOutput, calls=%fused_computation.2 | convolution fusion | flops 14453913600 | bytes 22579200 | tf_op jit(solution)/shard_map/dot_general | solution.py:29
  173.2 0.0 copy-start
  173.2 2.7 copy-done
  175.9 1.5 fusion.2
  177.4 0.0 all-gather.11.cloned.1.call-update
  177.4 2.1 convert_reduce_fusion
  179.5 22.9 %all-gather.2 = f32[8,5,112]{2,1,0:T(8,128)S(1)} all-gather(f32[1,5,112]{2,1,0:T(8,128)S(1)} %bitcast.53), channel_id=3, replica_groups=mesh['groups'=2,'tm'=8,'space'=2] {'tm'}, dimensions={0}, use_global_device_ids=true | all-gather | bytes 20160 | tf_op jit(solution)/shard_map/all_gather | solution.py:12
  202.5 24.3 %all-gather.11.cloned.1.call-done = f32[40,112,112]{2,1,0:T(8,128)} async-done(((f32[5,112,112]{2,1,0:T(8,128)}), f32[40,112,112]{2,1,0:T(8,128)}) %all-gather.11.cloned.1.call-update) | async-done | bytes 2007056 | tf_op jit(solution)/shard_map/all_gather | solution.py:12
  226.7 7.6 %while.16 = (s32[]{:T(128)}, f32[5,112,112]{2,1,0:T(8,128)S(1)}, f32[5,112]{1,0:T(8,128)S(1)}, s32[]{:T(128)}, f32[8,5,112,112]{3,2,1,0:T(8,128)}, /*index=5*/f32[8,5,112]{2,1,0:T(8,128)S(1)}, s32[]{:T(128)}, s32[]{:T(128)}) while((s32[]{:T(128)}, f32[5,112,112]{2,1,0:T(8,128)S(1)}, f32[5,112]{1,0:T(8,128)S(1)}, s32[]{:T(128)}, ...), condition=%wide.region_2.3_spmd.clone, body=%wide.region_1.2_spmd.clone.sunk | while | flops 189844 | bytes 759475 | solution.py:21
  226.7 1.0 add_select_fusion.4
  227.8 1.0 add_select_fusion.4
  228.9 1.0 add_select_fusion.4
  230.0 1.0 add_select_fusion.4
  231.1 1.0 add_select_fusion.4
  232.2 1.0 add_select_fusion.4
  233.3 1.0 add_select_fusion.4
  234.4 0.0 copy-start.1
  234.4 2.6 fusion.5
  237.1 0.0 copy-done.1
  237.1 2.4 fusion
  239.5 8.0 %reshape.34 = bf16[2,12,80,560]{2,1,0,3:T(8,128)(2,1)} reshape(bf16[1920,5,112]{0,2,1:T(8,128)(2,1)S(1)} %fusion) | data formatting | bytes 4300800 | tf_op jit(solution)/shard_map/reshape | solution.py:75
  247.5 6.0 %copy.16 = bf16[2,12,80,560]{3,2,0,1:T(8,128)(2,1)S(1)} copy(bf16[2,12,80,560]{2,1,0,3:T(8,128)(2,1)} %reshape.34) | data formatting | bytes 4300800 | tf_op jit(solution)/shard_map/reshape | solution.py:75
  253.5 6.6 %all_to_all.18 = bf16[2,12,80,560]{3,2,0,1:T(8,128)(2,1)S(1)} all-to-all(bf16[2,12,80,560]{3,2,0,1:T(8,128)(2,1)S(1)} %copy.16), channel_id=1, replica_groups=mesh['groups'=2,'tm'=8,'space'=2] {'space'}, dimensions={1} | all-to-all | bytes 4300800 | tf_op jit(solution)/shard_map/all_to_all | solution.py:76
  260.1 2.5 copy.18
  262.6 2.9 %all_to_all.16 = bf16[2,6,80,1120]{3,2,1,0:T(8,128)(2,1)} reshape(bf16[2,6,80,2,560]{4,3,2,1,0:T(2,128)(2,1)S(1)} %copy.18) | data formatting | bytes 4300800 | tf_op jit(solution)/shard_map/all_to_all | solution.py:76
  (11 shorter events, 0.1 us)
Async XLA Ops:
  6.5 23.5 %all-gather.9.cloned.1.call-start = ((), (), s32[]{:S(2)}) async-start(), calls=%async_computation.2 | async-start | bytes 13271040 | tf_op jit(solution)/shard_map/all_gather | solution.py:66
  7.3 143.5 %all-gather.7.cloned.1.call-start = ((), (), s32[]{:S(2)}) async-start(), calls=%async_computation.1 | async-start | bytes 9031680 | tf_op jit(solution)/shard_map/all_gather | solution.py:33
  24.8 201.9 %all-gather.11.cloned.1.call-start = ((), (), s32[]{:S(2)}) async-start(), calls=%async_computation.3 | async-start | bytes 2580480 | tf_op jit(solution)/shard_map/all_gather | solution.py:12
  173.2 2.7 %copy-start = (bf16[1680,1920]{1,0:T(8,128)(2,1)}, bf16[1680,1920]{1,0:T(8,128)(2,1)S(1)}, u32[]{:S(2)}) copy-start(bf16[1680,1920]{1,0:T(8,128)(2,1)S(1)} %convolution_convert_fusion) | copy-start | bytes 19353604
  234.4 2.7 copy-start.1
Sparse Core Ops, SparseCore 0:
  8.9 21.0 all-gather.8
  32.2 118.5 all-gather.6
  177.5 49.1 all-gather.10
where the time goes:
time: 276 us; the launch traced here: 272 us
  waiting for transfers between devices  151 us (55%)
  local copies, waits for them, and re-layouts  39.6 us (14%)
  blocking collectives  29.5 us (11%)
  matrix products  28.9 us (10%)
  between operations  13.2 us (5%)
  other arithmetic  9.53 us (3%)
    all_gather x1, waiting for transfers between devices, project_rows(): return make_adder(flat, lax.all_gather(columns, 'tm', axis=0, tiled=True))  121 us
    all_gather x1, waiting for transfers between devices, entering(): pieces = jax.tree.map(lambda part: lax.all_gather(part, axis), value)  24.3 us
    all_gather x1, blocking collectives, entering(): pieces = jax.tree.map(lambda part: lax.all_gather(part, axis), value)  22.9 us
    dot_general x1, matrix products, make_adder(): return jnp.dot(flat, shard_rows, preferred_element_type=jnp.float32)  22.4 us
    reshape x2, local copies, waits for them, and re-layouts, on_device(): attended.reshape(frame_count, joined_rows, column_count, heads_here * HEAD)  14 us
    unnamed x5, local copies, waits for them, and re-layouts  8.94 us
    select_n x14, other arithmetic, hop(): jnp.where(position < mine, new, old)  7.4 us
    all_to_all x1, blocking collectives, on_device(): lax.all_to_all(attended, 'space', split_axis=1, concat_axis=3, tiled=True)  6.59 us
  transfers between devices with their start and end apart: 3, of which 3 were waited for; matrix products, arithmetic and copies ran while one was open for 7% of the time, Pallas kernels for 0%

commit v1 on v0

v1 whole, which is shorter than its diff:
```python
import functools

import jax
import jax.numpy as jnp
from jax import lax
from jax.experimental import pallas as pl
from jax.experimental.pallas import tpu as pltpu
from jax.sharding import PartitionSpec as P

HEADS = 10
HEAD = 112
LANES = 128
CLASSES = 3
MESH = pl.DeviceIdType.MESH


def round_plan(tiles):
    plan, first = [], 0
    while tiles - first >= 2 * CLASSES:
        plan.append((first, CLASSES))
        first += 2 * CLASSES
    while tiles - first > 0:
        plan.append((first, 2))
        first += 4
    return plan


def gather_kernel(plan, deep, wide, x_hbm, w_ref, p_ref, buf, x_vm, w_vm,
                  x_sem, own_sem, load_sem, zs, zr, ys, yr, xs, xr, cs, cr):
    group, t, core = lax.axis_index("groups"), lax.axis_index("tm"), lax.axis_index("space")
    z, y = t // wide, t % wide
    own_class = group % 2
    depth = w_ref.shape[0]
    x_peer = {"groups": group + 1 - 2 * own_class}
    y_peer = {"tm": z * wide + 1 - y}
    core_peer = {"space": 1 - core}

    def z_at(dz):
        return lax.rem(z + deep - dz, deep)

    barrier = pltpu.get_barrier_semaphore()
    peers = [x_peer, y_peer, core_peer]
    peers += [{"tm": lax.rem(z + dz, deep) * wide + y} for dz in range(1, deep)]
    for peer in peers:
        pl.semaphore_signal(barrier, inc=1, device_id=peer, device_id_type=MESH)

    x_copy = pltpu.make_async_copy(x_hbm, x_vm, x_sem)
    x_copy.start()

    def cols(r, kind, parity):
        return pl.ds(pl.multiple_of((plan[r][0] + 2 * kind + parity) * LANES, LANES), LANES)

    def rows(shard):
        return pl.ds(pl.multiple_of(shard * depth, 8), depth)

    def kind_of(s):
        return own_class if s == 0 else 2

    def fetched(r):
        return range(plan[r][1] - 1)

    own = {}
    for r, (first, kinds) in enumerate(plan):
        for kind in range(kinds):
            c = cols(r, kind, core)
            own[r, kind] = pltpu.make_async_copy(
                w_ref.at[:, c], buf.at[rows(t), c], own_sem.at[r, kind])
            own[r, kind].start()

    pl.semaphore_wait(barrier, len(peers))

    def remote(src, dst, send, recv, peer):
        return pltpu.make_async_remote_copy(
            src_ref=src, dst_ref=dst, send_sem=send, recv_sem=recv,
            device_id=peer, device_id_type=MESH)

    def z_copy(r, s, dz):
        c = cols(r, kind_of(s), core)
        return remote(w_ref.at[:, c], buf.at[rows(t), c], zs.at[r, s, dz], zr.at[r, s, dz],
                      {"tm": lax.rem(z + dz, deep) * wide + y})

    def y_copy(r, s, dz):
        c = cols(r, kind_of(s), core)
        at = buf.at[rows(z_at(dz) * wide + y), c]
        return remote(w_ref.at[:, c] if dz == 0 else at, at, ys.at[r, s, dz], yr.at[r, s, dz], y_peer)

    def x_copy_of(r, dz, side):
        c = cols(r, own_class, core)
        at = buf.at[rows(z_at(dz) * wide + (y if side == 0 else 1 - y)), c]
        return remote(at, at, xs.at[r, side, dz], xr.at[r, side, dz], x_peer)

    def core_copy(r, s):
        kind = own_class if s == 0 else (2 if s == 1 else 1 - own_class)
        at = buf.at[:, cols(r, kind, core)]
        return remote(at, at, cs.at[r, s], cr.at[r, s], core_peer)

    sent = []

    def start(copy):
        copy.start()
        sent.append(copy)

    def send_own(r):
        for s in fetched(r):
            for dz in range(1, deep):
                start(z_copy(r, s, dz))
        for s in fetched(r):
            start(y_copy(r, s, 0))

    def width(r):
        return 2 * plan[r][1] * LANES

    def load(r):
        return pltpu.make_async_copy(
            buf.at[:, pl.ds(plan[r][0] * LANES, width(r))],
            w_vm.at[r % 2, :, pl.ds(0, width(r))], load_sem.at[r % 2])

    step = 2 * LANES
    block = 240

    def multiply(r, piece):
        first = plan[r][0] * LANES + piece * step

        def body(i, carry):
            at = pl.ds(pl.multiple_of(i * block, block), block)
            p_ref[at, first:first + step] = jnp.dot(
                x_vm[at, :], w_vm[r % 2, :, piece * step:(piece + 1) * step],
                preferred_element_type=jnp.float32).astype(p_ref.dtype)
            return carry

        lax.fori_loop(0, x_vm.shape[0] // block, body, 0)

    rounds = len(plan)
    send_own(0)
    x_copy.wait()
    pending = []
    for r in range(rounds + 1):
        if r + 1 < rounds:
            send_own(r + 1)
        if r < rounds:
            for dz in range(1, deep):
                if pending:
                    multiply(*pending.pop(0))
                for s in fetched(r):
                    z_copy(r, s, dz).wait_recv()
                    start(y_copy(r, s, dz))
                    if s == 0:
                        start(x_copy_of(r, dz, 0))
            for dz in range(deep):
                for s in fetched(r):
                    y_copy(r, s, dz).wait_recv()
                    if s == 0:
                        start(x_copy_of(r, dz, 1))
            for kind in range(plan[r][1]):
                own[r, kind].wait()
            for s in fetched(r):
                start(core_copy(r, s))
        for item in pending:
            multiply(*item)
        pending = []
        if r >= 1:
            b = r - 1
            for dz in range(1, deep):
                x_copy_of(b, dz, 0).wait_recv()
            for dz in range(deep):
                x_copy_of(b, dz, 1).wait_recv()
            start(core_copy(b, 2))
            for s in list(fetched(b)) + [2]:
                core_copy(b, s).wait_recv()
            load(b).start()
            load(b).wait()
            pending = [(b, piece) for piece in range(plan[b][1])]
    for item in pending:
        multiply(*item)
    for copy in sent:
        copy.wait_send()


def gather_multiply(x, w, deep, wide):
    tokens, channels = x.shape
    depth, columns = w.shape
    plan = round_plan(columns // LANES)
    rounds = len(plan)
    dma = pltpu.SemaphoreType.DMA
    projected, _ = pl.pallas_call(
        functools.partial(gather_kernel, plan, deep, wide),
        out_shape=(jax.ShapeDtypeStruct((tokens, columns), jnp.bfloat16),
                   jax.ShapeDtypeStruct((channels, columns), jnp.bfloat16)),
        in_specs=[pl.BlockSpec(memory_space=pl.ANY), pl.BlockSpec(memory_space=pltpu.VMEM)],
        out_specs=(pl.BlockSpec(memory_space=pltpu.VMEM), pl.BlockSpec(memory_space=pl.ANY)),
        scratch_shapes=[
            pltpu.VMEM((tokens, channels), jnp.bfloat16),
            pltpu.VMEM((2, channels, 2 * CLASSES * LANES), jnp.bfloat16),
            dma, dma((rounds, CLASSES)), dma((2,)),
            dma((rounds, 2, deep)), dma((rounds, 2, deep)),
            dma((rounds, 2, deep)), dma((rounds, 2, deep)),
            dma((rounds, 2, deep)), dma((rounds, 2, deep)),
            dma((rounds, 3)), dma((rounds, 3)),
        ],
        compiler_params=pltpu.CompilerParams(
            collective_id=0, has_side_effects=True, vmem_limit_bytes=56 * 2 ** 20),
        name="gather_multiply",
    )(x, w)
    return projected


def own_share(states, key_sums):
    both = jnp.concatenate([states, key_sums[:, :, None]], axis=2)
    both = lax.psum(both, "space")
    pieces = lax.all_gather(both, "tm")
    place = lax.broadcasted_iota(jnp.int32, (pieces.shape[0], 1, 1, 1), 0)
    total = jnp.sum(jnp.where(place <= lax.axis_index("tm"), pieces, 0.0), axis=0)
    return total[:, :, :HEAD], total[:, :, HEAD]


def on_device(deep, wide, latents, proj_weight):
    frame_count, band_rows, column_count, channels = latents.shape
    flat = latents.reshape(-1, channels)
    depth, columns = proj_weight.shape
    part = HEADS * HEAD
    queries, keys, values = (proj_weight[:, i * part:(i + 1) * part] for i in range(3))
    if wide:
        room = -(-part // LANES) * LANES
        total = 2 * CLASSES * LANES * ((3 * room) // (2 * CLASSES * LANES))
        total += -(-(3 * room - total) // (4 * LANES)) * 4 * LANES
        gap = ((0, 0), (0, room - part))
        packed = jnp.concatenate(
            [jnp.pad(keys, gap), jnp.pad(values, gap), jnp.pad(queries, ((0, 0), (0, total - 2 * room - part)))], axis=1)
        projected = gather_multiply(flat, packed, deep, wide)
        keys, values, queries = (projected[:, i * room:i * room + part] for i in range(3))
    else:
        full = lax.all_gather(proj_weight, "tm", axis=0, tiled=True)
        projected = jnp.dot(flat, full, preferred_element_type=jnp.float32).astype(jnp.bfloat16)
        queries, keys, values = (projected[:, i * part:(i + 1) * part] for i in range(3))
    queries, keys, values = (a.reshape(-1, HEADS, HEAD) for a in (queries, keys, values))
    queries, keys = jax.nn.relu(queries), jax.nn.relu(keys)
    states = jnp.einsum("nhe,nhf->hef", keys, values, preferred_element_type=jnp.float32)
    key_sums = jnp.sum(keys, axis=0, dtype=jnp.float32)
    states, key_sums = own_share(states, key_sums)
    numerator = jnp.einsum(
        "nhe,hef->nhf", queries, states.astype(jnp.bfloat16), preferred_element_type=jnp.float32)
    denominator = jnp.einsum(
        "nhe,he->nh", queries.astype(jnp.float32), key_sums, precision=lax.Precision.HIGHEST)
    attended = (numerator / (denominator[:, :, None] + 1.0)).astype(jnp.bfloat16)
    return attended.reshape(frame_count, band_rows, column_count, part)


def solution(mesh):
    groups, blocks, bands = (mesh.shape[a] for a in ("groups", "tm", "space"))
    wide = 2

    def body(latents, proj_weight):
        fits = (groups == 2 and bands == 2 and blocks % wide == 0 and proj_weight.shape[0] % 8 == 0)
        return on_device(blocks // wide, wide if fits else 0, latents, proj_weight)

    return jax.shard_map(
        body,
        mesh=mesh,
        in_specs=(P(("groups", "tm"), "space", None, None), P("tm", None)),
        out_specs=P(("groups", "tm"), "space", None, None),
        check_vma=False,
    )
```

time: 276 us -> 277 us (level)
  Pallas kernels: 0 us -> 115 us
  waiting for transfers between devices: 151 us -> 95.6 us
  blocking collectives: 29.5 us -> 0 us
  matrix products: 28.9 us -> 5.64 us
  local copies, waits for them, and re-layouts: 39.6 us -> 27.9 us
  other arithmetic: 9.53 us -> 14.6 us
    pallas_call x0 -> x1, Pallas kernels: none -> 115 us  [gather_multiply(): pl.pallas_call(functools.partial(gather_kernel, plan, deep, wide), out_sh...]
    all_gather x3 -> x1, waiting for transfers between devices: 150 us -> 75.7 us  [own_share(): pieces = lax.all_gather(both, 'tm')]
    dot_general x4 -> x3, matrix products: 28.9 us -> 5.64 us  [the longest x1 2.4 us: on_device(): jnp.einsum('nhe,nhf->hef', keys, values, preferred_element_type=jnp.float32)]
    all_gather x1 -> x0, blocking collectives: 22.9 us -> none  [entering(): pieces = jax.tree.map(lambda part: lax.all_gather(part, axis), value)]
    psum x0 -> x1, waiting for transfers between devices: none -> 19.8 us  [own_share(): both = lax.psum(both, 'space')]
    unnamed x5 -> x2, local copies, waits for them, and re-layouts: 8.94 us -> 0.01 us
    select_n x14 -> x0, other arithmetic: 7.4 us -> none  [hop(): jnp.where(position < mine, new, old)]
    reshape x4 -> x2, local copies, waits for them, and re-layouts: 21.7 us -> 15 us  [on_device(): return attended.reshape(frame_count, band_rows, column_count, part)]
  transfers between devices with their start and end apart: 3 -> 2, of which waited for: 3 -> 2; matrix products, arithmetic and copies ran while one was open for 7% -> 1% of each run, Pallas kernels for 0% -> 0%
where the time goes in v1:
time: 277 us; the launch traced here: 272 us
  Pallas kernels  115 us (42%)
  waiting for transfers between devices  95.6 us (35%)
  local copies, waits for them, and re-layouts  27.9 us (10%)
  other arithmetic  14.6 us (5%)
  between operations  13.5 us (5%)
  matrix products  5.64 us (2%)
    pallas_call x1, Pallas kernels, gather_multiply(): pl.pallas_call(functools.partial(gather_kernel, plan, deep, wide), out_sh...  115 us
    all_gather x1, waiting for transfers between devices, own_share(): pieces = lax.all_gather(both, 'tm')  75.7 us
    psum x1, waiting for transfers between devices, own_share(): both = lax.psum(both, 'space')  19.8 us
    reshape x2, local copies, waits for them, and re-layouts, on_device(): return attended.reshape(frame_count, band_rows, column_count, part)  15 us
    max x1, other arithmetic, on_device(): queries, keys = (jax.nn.relu(queries), jax.nn.relu(keys))  5.98 us
    max x2, local copies, waits for them, and re-layouts, on_device(): queries, keys = (jax.nn.relu(queries), jax.nn.relu(keys))  5.93 us
  transfers between devices with their start and end apart: 2, of which 2 were waited for; matrix products, arithmetic and copies ran while one was open for 1% of the time, Pallas kernels for 0%

profile of v1, /device:TPU:25, one launch (start us, length us, event | category | flops | bytes accessed | tf_op | source)
XLA Modules:
  0.0 272.3 jit_solution(11219215956885503057)
XLA Ops:
  6.5 0.0 copy-start
  6.5 0.0 all-reduce.4.cloned.1.call-start
  6.5 1.9 fusion.7
  8.4 0.0 copy-done
  8.5 1.2 slice_select_fusion
  9.6 1.4 fusion.5.w_ref
  11.0 114.9 %gather_multiply.1 = (bf16[960,3584]{1,0:T(8,128)(2,1)}, bf16[2240,3584]{1,0:T(8,128)(2,1)}) custom-call(bf16[960,2240]{1,0:T(8,128)(2,1)} %bitcast.27, bf16[280,3584]{1,0:T(8,128)(2,1)} %fusion.5.w_ref), custom_call_target="tpu_custom_call" | custom-call | tf_op jit(solution)/shard_map/gather_multiply/pallas_call | solution.py:185
  125.9 6.0 %slice_maximum_fusion = (bf16[960,1120]{1,0:T(8,128)(2,1)}, bf16[960,1120]{1,0:T(8,128)(2,1)}, bf16[960,1120]{1,0:T(8,128)(2,1)}) fusion(bf16[960,3584]{1,0:T(8,128)(2,1)} %get-tuple-element.6), kind=kLoop, calls=%fused_computation.10 | loop fusion | flops 2150400 | bytes 12902400 | tf_op jit(solution)/shard_map/jit(relu)/max | solution.py:236
  131.9 2.1 convert_reduce_fusion
  134.0 3.0 %copy.24 = bf16[960,1120]{0,1:T(8,128)(2,1)S(1)} copy(bf16[960,1120]{1,0:T(8,128)(2,1)} %get-tuple-element.9) | data formatting | bytes 4300800 | tf_op jit(solution)/shard_map/jit(relu)/max | solution.py:236
  137.0 4.2 %copy.25 = bf16[960,1120]{0,1:T(8,128)(2,1)} copy(bf16[960,1120]{1,0:T(8,128)(2,1)} %get-tuple-element.8) | data formatting | bytes 4300800 | tf_op jit(solution)/shard_map/slice | solution.py:230
  141.2 0.4 broadcast_in_dim.19
  141.6 2.4 fusion.8
  144.0 1.0 maximum_bitcast_fusion
  145.1 0.0 all-reduce.4.cloned.1.call-update
  145.1 0.2 all-gather.2.cloned.1.call-start
  145.3 19.8 %all-reduce.4.cloned.1.call-done = f32[1,10,112,113]{3,2,1,0:T(8,128)} async-done(((f32[1,10,112,113]{3,2,1,0:T(8,128)}), f32[1,10,112,113]{3,2,1,0:T(8,128)}) %all-reduce.4.cloned.1.call-update) | async-done | bytes 506256 | tf_op jit(solution)/shard_map/psum | solution.py:209
  165.1 0.0 all-gather.2.cloned.1.call-update
  165.1 3.0 %copy.27 = bf16[960,1120]{0,1:T(8,128)(2,1)S(1)} copy(bf16[960,1120]{1,0:T(8,128)(2,1)} %get-tuple-element.7) | data formatting | bytes 4300800 | tf_op jit(solution)/shard_map/jit(relu)/max | solution.py:236
  168.1 75.7 %all-gather.2.cloned.1.call-done = f32[8,10,112,113]{3,2,1,0:T(8,128)} async-done(((f32[1,10,112,113]{3,2,1,0:T(8,128)}), f32[8,10,112,113]{3,2,1,0:T(8,128)}) %all-gather.2.cloned.1.call-update) | async-done | bytes 4049936 | tf_op jit(solution)/shard_map/all_gather | solution.py:210
  243.9 2.9 %select_reduce_fusion = f32[10,112,113]{2,1,0:T(8,128)S(1)} fusion(f32[8,10,112,113]{3,2,1,0:T(8,128)} %all-gather.2.cloned.1.call-done, pred[8]{0:T(512)(128)(4,1)S(1)} %iota_compare_fusion.3), kind=kLoop, calls=%fused_computation.4 | loop fusion | flops 1898400 | bytes 4556168 | tf_op jit(solution)/shard_map/reduce_sum | solution.py:212
  246.8 0.4 slice_reduce_fusion
  247.2 1.0 fusion.9
  248.2 2.2 fusion
  250.5 8.7 %reshape.31 = bf16[2,6,80,1120]{2,1,0,3:T(8,128)(2,1)} reshape(bf16[960,10,112]{0,2,1:T(8,128)(2,1)} %fusion) | data formatting | bytes 4300800 | tf_op jit(solution)/shard_map/reshape | solution.py:245
  259.1 6.4 %copy.33 = bf16[2,6,80,1120]{3,2,1,0:T(8,128)(2,1)} copy(bf16[2,6,80,1120]{2,1,0,3:T(8,128)(2,1)} %reshape.31) | data formatting | bytes 4300800 | tf_op jit(solution)/shard_map/reshape | solution.py:245
  (3 shorter events, 0.0 us)
Async XLA Ops:
  6.5 1.9 copy-start
  6.5 158.6 %all-reduce.4.cloned.1.call-start = ((), (), s32[]{:S(2)}) async-start(), calls=%async_computation | async-start | bytes 1146880 | tf_op jit(solution)/shard_map/psum | solution.py:209
  145.1 98.8 %all-gather.2.cloned.1.call-start = ((), (), s32[]{:S(2)}) async-start(), calls=%async_computation.1 | async-start | bytes 5160960 | tf_op jit(solution)/shard_map/all_gather | solution.py:210
Sparse Core Ops, SparseCore 0:
  145.2 19.8 all-reduce.3
  167.3 76.5 all-gather.1

commit v2 on v1

--- a/solution.py
+++ b/solution.py
@@ -25,8 +25,9 @@
     return plan
 
 
-def gather_kernel(plan, deep, wide, x_hbm, w_ref, p_ref, buf, x_vm, w_vm,
-                  x_sem, own_sem, load_sem, zs, zr, ys, yr, xs, xr, cs, cr):
+def gather_kernel(plan, deep, wide, room, x_hbm, w_ref, o_ref, buf, x_vm, w_vm, p_ref,
+                  local, from_core, block_sum, from_y, pair_sum, from_z, to_y, totals, rounded,
+                  x_sem, own_sem, load_sem, zs, zr, ys, yr, xs, xr, cs, cr, ss, sr):
     group, t, core = lax.axis_index("groups"), lax.axis_index("tm"), lax.axis_index("space")
     z, y = t // wide, t % wide
     own_class = group % 2
@@ -130,7 +131,111 @@
 
         lax.fori_loop(0, x_vm.shape[0] // block, body, 0)
 
+    tokens = x_vm.shape[0]
+    half = HEADS // 2
+    rows_half = HEAD // 2
+    my_heads, other_heads = pl.ds(core * half, half), pl.ds((1 - core) * half, half)
+    my_rows = pl.ds(pl.multiple_of(y * rows_half, 8), rows_half)
+    other_rows = pl.ds(pl.multiple_of((1 - y) * rows_half, 8), rows_half)
+
+    def block_states():
+        lane = lax.broadcasted_iota(jnp.int32, (block, LANES), 1)
+        for h in range(HEADS):
+            def body(i, total):
+                at = pl.ds(pl.multiple_of(i * block, block), block)
+                keys = jnp.maximum(p_ref[at, h * HEAD:h * HEAD + LANES], 0)
+                values = p_ref[at, room + h * HEAD:room + h * HEAD + LANES]
+                values = jnp.where(lane < HEAD, values, jnp.ones_like(values))
+                return total + lax.dot_general(
+                    keys, values, (((0,), (0,)), ((), ())), preferred_element_type=jnp.float32)
+
+            local[h] = lax.fori_loop(0, tokens // block, body, jnp.zeros((LANES, LANES), jnp.float32))[:HEAD]
+
+    def block_states_and_send():
+        block_states()
+        start(core_sum_copy())
+
+    def core_sum_copy():
+        return remote(local.at[other_heads], from_core, ss.at[0], sr.at[0], core_peer)
+
+    def y_sum_copy():
+        return remote(block_sum.at[:, other_rows], from_y, ss.at[1], sr.at[1], y_peer)
+
+    def z_sum_copy(dz):
+        return remote(pair_sum, from_z.at[dz], ss.at[3 + dz], sr.at[3 + dz],
+                      {"tm": lax.rem(z + dz, deep) * wide + y})
+
+    def y_total_copy():
+        return remote(to_y, totals.at[my_heads, my_rows], ss.at[2], sr.at[2], y_peer)
+
+    def core_total_copy():
+        return remote(totals.at[my_heads], totals.at[my_heads], ss.at[3], sr.at[3], core_peer)
+
+    def exchange_core():
+        core_sum_copy().wait_recv()
+        block_sum[...] = local[my_heads] + from_core[...]
+        start(y_sum_copy())
+
+    def exchange_y():
+        y_sum_copy().wait_recv()
+        pair_sum[...] = block_sum[:, my_rows] + from_y[...]
+        for dz in range(1, deep):
+            @pl.when(z + dz < deep)
+            def _():
+                z_sum_copy(dz).start()
+
+    def exchange_z():
+        earlier_me = block_sum[:, my_rows] + jnp.where(y == 0, 0.0, from_y[...])
+        earlier_peer = from_y[...] + jnp.where(y == 0, block_sum[:, my_rows], 0.0)
+        totals[my_heads, my_rows] = earlier_me
+        to_y[...] = earlier_peer
+        for dz in range(1, deep):
+            @pl.when(z >= dz)
+            def _():
+                z_sum_copy(dz).wait_recv()
+                totals[my_heads, my_rows] += from_z[dz]
+                to_y[...] += from_z[dz]
+        start(y_total_copy())
+
+    def exchange_back():
+        y_total_copy().wait_recv()
+        start(core_total_copy())
+
+    def attend():
+        core_total_copy().wait_recv()
+        lane = lax.broadcasted_iota(jnp.int32, (HEAD, LANES), 1)
+        for h in range(HEADS):
+            total = totals[h]
+            sums = jnp.broadcast_to(total[:, HEAD:HEAD + 1], (HEAD, LANES))
+            high = sums.astype(jnp.bfloat16).astype(jnp.float32)
+            middle = (sums - high).astype(jnp.bfloat16).astype(jnp.float32)
+            low = sums - high - middle
+            tail = jnp.where(lane == HEAD, high, jnp.where(lane == HEAD + 1, middle, jnp.where(lane == HEAD + 2, low, 0.0)))
+            rounded[h, :HEAD] = jnp.where(lane < HEAD, total, tail).astype(jnp.bfloat16)
+            rounded[h, HEAD:] = jnp.zeros((LANES - HEAD, LANES), jnp.bfloat16)
+
+        def body(i, carry):
+            at = pl.ds(pl.multiple_of(i * block, block), block)
+            for h in range(HEADS):
+                first = 2 * room + h * HEAD
+                queries = jnp.maximum(p_ref[at, first:first + LANES], 0)
+                out = jnp.dot(queries, rounded[h], preferred_element_type=jnp.float32)
+                below = out[:, HEAD:HEAD + 1] + out[:, HEAD + 1:HEAD + 2] + out[:, HEAD + 2:HEAD + 3] + 1.0
+                o_ref[at, h * HEAD:(h + 1) * HEAD] = (out[:, :HEAD] / below).astype(o_ref.dtype)
+            return carry
+
+        lax.fori_loop(0, tokens // block, body, 0)
+
     rounds = len(plan)
+    last_kv = [2 * room <= plan[r][0] * LANES + width(r) for r in range(rounds)].index(True)
+    stages = [block_states_and_send, exchange_core, exchange_y, exchange_z, exchange_back]
+    done = []
+
+    def advance():
+        if len(stages) > len(done):
+            stages[len(done)]()
+            done.append(1)
+
     send_own(0)
     x_copy.wait()
     pending = []
@@ -158,6 +263,8 @@
         for item in pending:
             multiply(*item)
         pending = []
+        if r - 2 >= last_kv:
+            advance()
         if r >= 1:
             b = r - 1
             for dz in range(1, deep):
@@ -168,40 +275,61 @@
             for s in list(fetched(b)) + [2]:
                 core_copy(b, s).wait_recv()
             load(b).start()
+            if r - 2 >= last_kv:
+                advance()
             load(b).wait()
             pending = [(b, piece) for piece in range(plan[b][1])]
     for item in pending:
         multiply(*item)
+    for _ in stages:
+        advance()
+    attend()
+    for dz in range(1, deep):
+        @pl.when(z + dz < deep)
+        def _():
+            z_sum_copy(dz).wait_send()
     for copy in sent:
         copy.wait_send()
 
 
-def gather_multiply(x, w, deep, wide):
+def gather_multiply(x, w, deep, wide, room):
     tokens, channels = x.shape
     depth, columns = w.shape
     plan = round_plan(columns // LANES)
     rounds = len(plan)
     dma = pltpu.SemaphoreType.DMA
-    projected, _ = pl.pallas_call(
-        functools.partial(gather_kernel, plan, deep, wide),
-        out_shape=(jax.ShapeDtypeStruct((tokens, columns), jnp.bfloat16),
+    half, f32 = HEADS // 2, jnp.float32
+    attended, _ = pl.pallas_call(
+        functools.partial(gather_kernel, plan, deep, wide, room),
+        out_shape=(jax.ShapeDtypeStruct((tokens, HEADS * HEAD), jnp.bfloat16),
                    jax.ShapeDtypeStruct((channels, columns), jnp.bfloat16)),
         in_specs=[pl.BlockSpec(memory_space=pl.ANY), pl.BlockSpec(memory_space=pltpu.VMEM)],
         out_specs=(pl.BlockSpec(memory_space=pltpu.VMEM), pl.BlockSpec(memory_space=pl.ANY)),
         scratch_shapes=[
             pltpu.VMEM((tokens, channels), jnp.bfloat16),
             pltpu.VMEM((2, channels, 2 * CLASSES * LANES), jnp.bfloat16),
+            pltpu.VMEM((tokens, columns), jnp.bfloat16),
+            pltpu.VMEM((HEADS, HEAD, LANES), f32),
+            pltpu.VMEM((half, HEAD, LANES), f32),
+            pltpu.VMEM((half, HEAD, LANES), f32),
+            pltpu.VMEM((half, HEAD // 2, LANES), f32),
+            pltpu.VMEM((half, HEAD // 2, LANES), f32),
+            pltpu.VMEM((deep, half, HEAD // 2, LANES), f32),
+            pltpu.VMEM((half, HEAD // 2, LANES), f32),
+            pltpu.VMEM((HEADS, HEAD, LANES), f32),
+            pltpu.VMEM((HEADS, LANES, LANES), jnp.bfloat16),
             dma, dma((rounds, CLASSES)), dma((2,)),
             dma((rounds, 2, deep)), dma((rounds, 2, deep)),
             dma((rounds, 2, deep)), dma((rounds, 2, deep)),
             dma((rounds, 2, deep)), dma((rounds, 2, deep)),
             dma((rounds, 3)), dma((rounds, 3)),
+            dma((deep + 3,)), dma((deep + 3,)),
         ],
         compiler_params=pltpu.CompilerParams(
             collective_id=0, has_side_effects=True, vmem_limit_bytes=56 * 2 ** 20),
         name="gather_multiply",
     )(x, w)
-    return projected
+    return attended
 
 
 def own_share(states, key_sums):
@@ -226,12 +354,11 @@
         gap = ((0, 0), (0, room - part))
         packed = jnp.concatenate(
             [jnp.pad(keys, gap), jnp.pad(values, gap), jnp.pad(queries, ((0, 0), (0, total - 2 * room - part)))], axis=1)
-        projected = gather_multiply(flat, packed, deep, wide)
-        keys, values, queries = (projected[:, i * room:i * room + part] for i in range(3))
-    else:
-        full = lax.all_gather(proj_weight, "tm", axis=0, tiled=True)
-        projected = jnp.dot(flat, full, preferred_element_type=jnp.float32).astype(jnp.bfloat16)
-        queries, keys, values = (projected[:, i * part:(i + 1) * part] for i in range(3))
+        attended = gather_multiply(flat, packed, deep, wide, room)
+        return attended.reshape(frame_count, band_rows, column_count, part)
+    full = lax.all_gather(proj_weight, "tm", axis=0, tiled=True)
+    projected = jnp.dot(flat, full, preferred_element_type=jnp.float32).astype(jnp.bfloat16)
+    queries, keys, values = (projected[:, i * part:(i + 1) * part] for i in range(3))
     queries, keys, values = (a.reshape(-1, HEADS, HEAD) for a in (queries, keys, values))
     queries, keys = jax.nn.relu(queries), jax.nn.relu(keys)
     states = jnp.einsum("nhe,nhf->hef", keys, values, preferred_element_type=jnp.float32)

time: 277 us -> 155 us (0.56); the launches traced: 272 us -> 154 us
  waiting for transfers between devices: 95.6 us -> 0 us
  Pallas kernels: 115 us -> 147 us
  local copies, waits for them, and re-layouts: 27.9 us -> 5.04 us
  between operations: 13.5 us -> 0.02 us
  other arithmetic: 14.6 us -> 2.59 us
  matrix products: 5.64 us -> 0 us
    all_gather x1 -> x0, waiting for transfers between devices: 75.7 us -> none  [own_share(): pieces = lax.all_gather(both, 'tm')]
    pallas_call x1, Pallas kernels: 115 us -> 147 us  [gather_multiply(): pl.pallas_call(functools.partial(gather_kernel, plan, deep, wide, room),...]
    psum x1 -> x0, waiting for transfers between devices: 19.8 us -> none  [own_share(): both = lax.psum(both, 'space')]
    reshape x2 -> x0, local copies, waits for them, and re-layouts: 15 us -> none  [on_device(): return attended.reshape(frame_count, band_rows, column_count, part)]
    max x1 -> x0, other arithmetic: 5.98 us -> none  [on_device(): queries, keys = (jax.nn.relu(queries), jax.nn.relu(keys))]
    max x2 -> x0, local copies, waits for them, and re-layouts: 5.93 us -> none  [on_device(): queries, keys = (jax.nn.relu(queries), jax.nn.relu(keys))]
    dot_general x3 -> x0, matrix products: 5.64 us -> none  [the longest x1 2.4 us: on_device(): jnp.einsum('nhe,nhf->hef', keys, values, preferred_element_type=jnp.float32)]
    reduce_sum x2 -> x0, other arithmetic: 5.01 us -> none  [the longest x1 2.89 us: own_share(): jnp.sum(jnp.where(place <= lax.axis_index('tm'), pieces, 0.0), axis=0)]
  transfers between devices with their start and end apart: 2 -> 0, of which waited for: 2 -> 0; matrix products, arithmetic and copies ran while one was open for 1% -> 0% of each run, Pallas kernels for 0% -> 0%
where the time goes in v2:
time: 155 us; the launch traced here: 154 us
  Pallas kernels  147 us (95%)
  local copies, waits for them, and re-layouts  5.04 us (3%)
  other arithmetic  2.59 us (2%)
    pallas_call x1, Pallas kernels, gather_multiply(): pl.pallas_call(functools.partial(gather_kernel, plan, deep, wide, room),...  147 us
    unnamed x1, local copies, waits for them, and re-layouts  3.15 us

profile of v2, /device:TPU:25, one launch (start us, length us, event | category | flops | bytes accessed | tf_op | source)
XLA Modules:
  0.0 154.2 jit_solution(6945617392092422677)
XLA Ops:
  0.0 1.2 slice_select_fusion
  1.2 1.9 %fusion.5 = (bf16[280,1120]{1,0:T(8,128)(2,1)S(1)}, bf16[280,1120]{1,0:T(8,128)(2,1)S(1)}) fusion(bf16[280,3360]{1,0:T(8,128)(2,1)} %param.3), kind=kLoop, calls=%fused_computation.9 | loop fusion | bytes 2508800 | tf_op jit(solution)/shard_map/slice | solution.py:349
  3.1 1.4 fusion.4.w_ref
  4.5 146.5 %gather_multiply.1 = (bf16[960,1120]{1,0:T(8,128)(2,1)}, bf16[2240,3584]{1,0:T(8,128)(2,1)}) custom-call(bf16[960,2240]{1,0:T(8,128)(2,1)} %bitcast.2, bf16[280,3584]{1,0:T(8,128)(2,1)} %fusion.4.w_ref), custom_call_target="tpu_custom_call" | custom-call | tf_op jit(solution)/shard_map/gather_multiply/pallas_call | solution.py:302
  151.0 3.1 %copy.4 = bf16[2,6,80,1120]{3,2,1,0:T(8,128)(2,1)} copy(bf16[2,6,80,1120]{3,2,1,0:T(8,128)(2,1)} %bitcast.3) | data formatting | bytes 4300800

commit v3 on v2

v3 whole, which is shorter than its diff:
```python
import functools

import jax
import jax.numpy as jnp
from jax import lax
from jax.experimental import pallas as pl
from jax.experimental.pallas import tpu as pltpu
from jax.sharding import PartitionSpec as P

HEADS = 10
HEAD = 112
LANES = 128
MESH = pl.DeviceIdType.MESH


def unit_plan(units, early):
    split = units // 3
    split_early = early * 3 // 10
    both_early = early - 2 * split_early
    pairs = [2 * m if m < split_early else early + 2 * (m - split_early) for m in range(split)]
    both = [2 * split_early + m for m in range(both_early)]
    both += list(range(early + 2 * (split - split_early), units))
    order = [("mine", m) for m in range(split_early)] + [("both", m) for m in range(both_early)]
    order += [("mine", m) for m in range(split_early, split)] + [("both", m) for m in range(both_early, len(both))]
    return pairs, both, order


def gather_kernel(plan, early, deep, wide, x_hbm, w_ref, o_ref, buf, x_vm, w_vm, q_ref,
                  local, from_core, block_sum, from_y, pair_sum, from_z, to_y, totals, rounded,
                  x_sem, own_sem, load_sem, zs, zr, ys, yr, xs, xr, cs, cr, ss, sr):
    group, t, core = lax.axis_index("groups"), lax.axis_index("tm"), lax.axis_index("space")
    z, y = t // wide, t % wide
    own_class = group % 2
    depth = w_ref.shape[0]
    x_peer = {"groups": group + 1 - 2 * own_class}
    y_peer = {"tm": z * wide + 1 - y}
    core_peer = {"space": 1 - core}

    def z_at(dz):
        return lax.rem(z + deep - dz, deep)

    barrier = pltpu.get_barrier_semaphore()
    peers = [x_peer, y_peer, core_peer]
    peers += [{"tm": lax.rem(z + dz, deep) * wide + y} for dz in range(1, deep)]
    for peer in peers:
        pl.semaphore_signal(barrier, inc=1, device_id=peer, device_id_type=MESH)

    x_copy = pltpu.make_async_copy(x_hbm, x_vm, x_sem)
    x_copy.start()

    pairs, both, order = plan
    units = 2 * len(pairs) + len(both)
    step = 2 * LANES
    depth_of_split = len(pairs)

    def unit(kind, m):
        if kind == "both":
            return both[m]
        return pairs[m] + (own_class if kind == "mine" else 1 - own_class)

    def slot(kind, m):
        return {"mine": 0, "both": depth_of_split, "other": depth_of_split + len(both)}[kind] + m

    def cols(kind, m):
        return pl.ds(pl.multiple_of(unit(kind, m) * step + core * LANES, LANES), LANES)

    def rows(shard):
        return pl.ds(pl.multiple_of(shard * depth, 8), depth)

    everything = order + [("other", m) for m in range(depth_of_split)]

    def own_copy(kind, m):
        c = cols(kind, m)
        return pltpu.make_async_copy(w_ref.at[:, c], buf.at[rows(t), c], own_sem.at[slot(kind, m)])

    for tile in everything:
        own_copy(*tile).start()

    pl.semaphore_wait(barrier, len(peers))

    def remote(src, dst, send, recv, peer):
        return pltpu.make_async_remote_copy(
            src_ref=src, dst_ref=dst, send_sem=send, recv_sem=recv,
            device_id=peer, device_id_type=MESH)

    def z_copy(kind, m, dz):
        c, n = cols(kind, m), slot(kind, m)
        return remote(w_ref.at[:, c], buf.at[rows(t), c], zs.at[n, dz], zr.at[n, dz],
                      {"tm": lax.rem(z + dz, deep) * wide + y})

    def y_copy(kind, m, dz):
        c, n = cols(kind, m), slot(kind, m)
        at = buf.at[rows(z_at(dz) * wide + y), c]
        return remote(w_ref.at[:, c] if dz == 0 else at, at, ys.at[n, dz], yr.at[n, dz], y_peer)

    def x_pass(m, dz, side):
        at = buf.at[rows(z_at(dz) * wide + (y if side == 0 else 1 - y)), cols("mine", m)]
        return remote(at, at, xs.at[m, side, dz], xr.at[m, side, dz], x_peer)

    def core_pass(kind, m):
        at, n = buf.at[:, cols(kind, m)], slot(kind, m)
        return remote(at, at, cs.at[n], cr.at[n], core_peer)

    sent = []

    def start(copy):
        copy.start()
        sent.append(copy)

    def load(kind, m):
        n = slot(kind, m)
        c = pl.ds(pl.multiple_of(unit(kind, m) * step, step), step)
        return pltpu.make_async_copy(buf.at[:, c], w_vm.at[n], load_sem.at[n])

    block = 240

    tokens = x_vm.shape[0]
    half = HEADS // 2
    rows_half = HEAD // 2
    my_heads, other_heads = pl.ds(core * half, half), pl.ds((1 - core) * half, half)
    my_rows = pl.ds(pl.multiple_of(y * rows_half, 8), rows_half)
    other_rows = pl.ds(pl.multiple_of((1 - y) * rows_half, 8), rows_half)

    lane_of = lax.broadcasted_iota(jnp.int32, (block, LANES), 1)

    def multiply(kind, m):
        n, u = slot(kind, m), unit(kind, m)

        def project(i):
            at = pl.ds(pl.multiple_of(i * block, block), block)
            return at, jnp.dot(x_vm[at, :], w_vm[n], preferred_element_type=jnp.float32).astype(jnp.bfloat16)

        def keys_values(i, total):
            _, both_parts = project(i)
            keys = jnp.maximum(both_parts[:, :LANES], 0)
            values = both_parts[:, LANES:]
            values = jnp.where(lane_of < HEAD, values, jnp.ones_like(values))
            return total + lax.dot_general(
                keys, values, (((0,), (0,)), ((), ())), preferred_element_type=jnp.float32)

        def queries(i, carry):
            at, part = project(i)
            q_ref[u - early, at, :] = jnp.maximum(part, 0)
            return carry

        is_early = m < (sum(p < early for p in pairs) if kind != "both" else sum(p < early for p in both))
        if is_early:
            total = lax.fori_loop(0, tokens // block, keys_values, jnp.zeros((LANES, LANES), jnp.float32))
            local[u] = total[:HEAD]
        else:
            lax.fori_loop(0, tokens // block, queries, 0)

    def block_states_and_send():
        start(core_sum_copy())

    def core_sum_copy():
        return remote(local.at[other_heads], from_core, ss.at[0], sr.at[0], core_peer)

    def y_sum_copy():
        return remote(block_sum.at[:, other_rows], from_y, ss.at[1], sr.at[1], y_peer)

    def z_sum_copy(dz):
        return remote(pair_sum, from_z.at[dz], ss.at[3 + dz], sr.at[3 + dz],
                      {"tm": lax.rem(z + dz, deep) * wide + y})

    def y_total_copy():
        return remote(to_y, totals.at[my_heads, my_rows], ss.at[2], sr.at[2], y_peer)

    def core_total_copy():
        return remote(totals.at[my_heads], totals.at[my_heads], ss.at[3], sr.at[3], core_peer)

    def exchange_core():
        core_sum_copy().wait_recv()
        block_sum[...] = local[my_heads] + from_core[...]
        start(y_sum_copy())

    def exchange_y():
        y_sum_copy().wait_recv()
        pair_sum[...] = block_sum[:, my_rows] + from_y[...]
        for dz in range(1, deep):
            @pl.when(z + dz < deep)
            def _():
                z_sum_copy(dz).start()

    def exchange_z():
        earlier_me = block_sum[:, my_rows] + jnp.where(y == 0, 0.0, from_y[...])
        earlier_peer = from_y[...] + jnp.where(y == 0, block_sum[:, my_rows], 0.0)
        totals[my_heads, my_rows] = earlier_me
        to_y[...] = earlier_peer
        for dz in range(1, deep):
            @pl.when(z >= dz)
            def _():
                z_sum_copy(dz).wait_recv()
                totals[my_heads, my_rows] += from_z[dz]
                to_y[...] += from_z[dz]
        start(y_total_copy())

    def exchange_back():
        y_total_copy().wait_recv()
        start(core_total_copy())

    def attend():
        core_total_copy().wait_recv()
        lane = lax.broadcasted_iota(jnp.int32, (HEAD, LANES), 1)
        for h in range(HEADS):
            total = totals[h]
            sums = jnp.broadcast_to(total[:, HEAD:HEAD + 1], (HEAD, LANES))
            high = sums.astype(jnp.bfloat16).astype(jnp.float32)
            middle = (sums - high).astype(jnp.bfloat16).astype(jnp.float32)
            low = sums - high - middle
            tail = jnp.where(lane == HEAD, high, jnp.where(lane == HEAD + 1, middle, jnp.where(lane == HEAD + 2, low, 0.0)))
            rounded[h, :HEAD] = jnp.where(lane < HEAD, total, tail).astype(jnp.bfloat16)

        def body(i, carry):
            at = pl.ds(pl.multiple_of(i * block, block), block)
            for h in range(HEADS):
                first, last = h * HEAD, h * HEAD + HEAD
                head = first // step
                if last <= (head + 1) * step:
                    queries = q_ref[head, at, first - head * step:last - head * step]
                else:
                    queries = jnp.concatenate(
                        [q_ref[head, at, first - head * step:], q_ref[head + 1, at, :last - (head + 1) * step]], axis=1)
                out = jnp.dot(queries, rounded[h, :HEAD], preferred_element_type=jnp.float32)
                below = out[:, HEAD:HEAD + 1] + out[:, HEAD + 1:HEAD + 2] + out[:, HEAD + 2:HEAD + 3] + 1.0
                o_ref[at, h * HEAD:(h + 1) * HEAD] = (out[:, :HEAD] / below).astype(o_ref.dtype)
            return carry

        lax.fori_loop(0, tokens // block, body, 0)

    events = []

    def event(when, action):
        events.append((when, len(events), action))

    tile_time, hop = 6.3, 2.5

    def send_own(tile):
        for dz in range(1, deep):
            start(z_copy(*tile, dz))
        start(y_copy(*tile, 0))

    def from_z_tile(tile, dz):
        z_copy(*tile, dz).wait_recv()
        start(y_copy(*tile, dz))
        if tile[0] == "mine":
            start(x_pass(tile[1], dz, 0))

    def from_y_tile(tile, dz):
        y_copy(*tile, dz).wait_recv()
        if tile[0] == "mine":
            start(x_pass(tile[1], dz, 1))

    def from_x_tile(m, dz, side):
        x_pass(m, dz, side).wait_recv()

    def to_core(tile):
        own_copy(*tile).wait()
        start(core_pass(*tile))

    def from_core_tile(tile):
        core_pass(*tile).wait_recv()
        load(*tile).start()

    def run(tile):
        load(*tile).wait()
        multiply(*tile)

    def finish(tile, when):
        event(when, functools.partial(to_core, tile))
        event(when + hop, functools.partial(from_core_tile, tile))
        event(when + 2 * hop, functools.partial(run, tile))
        is_kv = tile[1] < (sum(p < early for p in (both if tile[0] == "both" else pairs)))
        return when + 2 * hop if is_kv else 0.0

    ready, x_end = 0.0, 0.0
    for i, tile in enumerate(order):
        base = i * tile_time
        event(max(base - 2 * tile_time, -1.0), functools.partial(send_own, tile))
        for dz in range(1, deep):
            event(base + dz * tile_time / (deep - 1), functools.partial(from_z_tile, tile, dz))
        for dz in range(deep):
            event(base + dz * tile_time / (deep - 1) + hop, functools.partial(from_y_tile, tile, dz))
        complete = base + tile_time + hop
        ready = max(ready, finish(tile, complete + 0.1))
        if tile[0] == "mine":
            x_end = max(x_end + 11.5, complete + 4.0)
            for dz in range(1, deep):
                event(x_end - 0.1, functools.partial(from_x_tile, tile[1], dz, 0))
            for dz in range(deep):
                event(x_end - 0.1, functools.partial(from_x_tile, tile[1], dz, 1))
            ready = max(ready, finish(("other", tile[1]), x_end))
    for stage, delay in ((block_states_and_send, 0.1), (exchange_core, 2.0), (exchange_y, 6.0),
                         (exchange_z, 18.0), (exchange_back, 22.0)):
        event(ready + delay, stage)
    events.sort(key=lambda e: e[:2])
    x_copy.wait()
    for _, _, action in events:
        action()
    attend()
    for dz in range(1, deep):
        @pl.when(z + dz < deep)
        def _():
            z_sum_copy(dz).wait_send()
    for copy in sent:
        copy.wait_send()


def gather_multiply(x, w, deep, wide, early):
    tokens, channels = x.shape
    depth, columns = w.shape
    step = 2 * LANES
    units = columns // step
    plan = unit_plan(units, early)
    split, fetched = len(plan[0]), len(plan[2])
    dma = pltpu.SemaphoreType.DMA
    half, f32 = HEADS // 2, jnp.float32
    attended, _ = pl.pallas_call(
        functools.partial(gather_kernel, plan, early, deep, wide),
        out_shape=(jax.ShapeDtypeStruct((tokens, HEADS * HEAD), jnp.bfloat16),
                   jax.ShapeDtypeStruct((channels, columns), jnp.bfloat16)),
        in_specs=[pl.BlockSpec(memory_space=pl.ANY), pl.BlockSpec(memory_space=pltpu.VMEM)],
        out_specs=(pl.BlockSpec(memory_space=pltpu.VMEM), pl.BlockSpec(memory_space=pl.ANY)),
        scratch_shapes=[
            pltpu.VMEM((tokens, channels), jnp.bfloat16),
            pltpu.VMEM((units, channels, step), jnp.bfloat16),
            pltpu.VMEM((units - early, tokens, step), jnp.bfloat16),
            pltpu.VMEM((HEADS, HEAD, LANES), f32),
            pltpu.VMEM((half, HEAD, LANES), f32),
            pltpu.VMEM((half, HEAD, LANES), f32),
            pltpu.VMEM((half, HEAD // 2, LANES), f32),
            pltpu.VMEM((half, HEAD // 2, LANES), f32),
            pltpu.VMEM((deep, half, HEAD // 2, LANES), f32),
            pltpu.VMEM((half, HEAD // 2, LANES), f32),
            pltpu.VMEM((HEADS, HEAD, LANES), f32),
            pltpu.VMEM((HEADS, HEAD, LANES), jnp.bfloat16),
            dma, dma((units,)), dma((units,)),
            dma((fetched, deep)), dma((fetched, deep)),
            dma((fetched, deep)), dma((fetched, deep)),
            dma((split, 2, deep)), dma((split, 2, deep)),
            dma((units,)), dma((units,)),
            dma((deep + 3,)), dma((deep + 3,)),
        ],
        compiler_params=pltpu.CompilerParams(
            collective_id=0, has_side_effects=True, vmem_limit_bytes=56 * 2 ** 20),
        name="gather_multiply",
    )(x, w)
    return attended


def own_share(states, key_sums):
    both = jnp.concatenate([states, key_sums[:, :, None]], axis=2)
    both = lax.psum(both, "space")
    pieces = lax.all_gather(both, "tm")
    place = lax.broadcasted_iota(jnp.int32, (pieces.shape[0], 1, 1, 1), 0)
    total = jnp.sum(jnp.where(place <= lax.axis_index("tm"), pieces, 0.0), axis=0)
    return total[:, :, :HEAD], total[:, :, HEAD]


def on_device(deep, wide, latents, proj_weight):
    frame_count, band_rows, column_count, channels = latents.shape
    flat = latents.reshape(-1, channels)
    depth, columns = proj_weight.shape
    part = HEADS * HEAD
    queries, keys, values = (proj_weight[:, i * part:(i + 1) * part] for i in range(3))
    if wide:
        gap = ((0, 0), (0, 0), (0, LANES - HEAD))
        pads = [jnp.pad(a.reshape(depth, HEADS, HEAD), gap) for a in (keys, values)]
        heads = jnp.stack(pads, axis=2).reshape(depth, 2 * HEADS * LANES)
        step = 2 * LANES
        rest = -(-part // step) * step
        packed = jnp.concatenate([heads, jnp.pad(queries, ((0, 0), (0, rest - part)))], axis=1)
        attended = gather_multiply(flat, packed, deep, wide, HEADS)
        return attended.reshape(frame_count, band_rows, column_count, part)
    full = lax.all_gather(proj_weight, "tm", axis=0, tiled=True)
    projected = jnp.dot(flat, full, preferred_element_type=jnp.float32).astype(jnp.bfloat16)
    queries, keys, values = (projected[:, i * part:(i + 1) * part] for i in range(3))
    queries, keys, values = (a.reshape(-1, HEADS, HEAD) for a in (queries, keys, values))
    queries, keys = jax.nn.relu(queries), jax.nn.relu(keys)
    states = jnp.einsum("nhe,nhf->hef", keys, values, preferred_element_type=jnp.float32)
    key_sums = jnp.sum(keys, axis=0, dtype=jnp.float32)
    states, key_sums = own_share(states, key_sums)
    numerator = jnp.einsum(
        "nhe,hef->nhf", queries, states.astype(jnp.bfloat16), preferred_element_type=jnp.float32)
    denominator = jnp.einsum(
        "nhe,he->nh", queries.astype(jnp.float32), key_sums, precision=lax.Precision.HIGHEST)
    attended = (numerator / (denominator[:, :, None] + 1.0)).astype(jnp.bfloat16)
    return attended.reshape(frame_count, band_rows, column_count, part)


def solution(mesh):
    groups, blocks, bands = (mesh.shape[a] for a in ("groups", "tm", "space"))
    wide = 2

    def body(latents, proj_weight):
        fits = (groups == 2 and bands == 2 and blocks % wide == 0 and proj_weight.shape[0] % 8 == 0)
        return on_device(blocks // wide, wide if fits else 0, latents, proj_weight)

    return jax.shard_map(
        body,
        mesh=mesh,
        in_specs=(P(("groups", "tm"), "space", None, None), P("tm", None)),
        out_specs=P(("groups", "tm"), "space", None, None),
        check_vma=False,
    )
```

time: 155 us -> 146 us (0.942)
  Pallas kernels: 147 us -> 130 us
  local copies, waits for them, and re-layouts: 5.04 us -> 9.03 us
  other arithmetic: 2.59 us -> 4.74 us
    pallas_call x1, Pallas kernels: 147 us -> 130 us  [gather_multiply(): pl.pallas_call(functools.partial(gather_kernel, plan, early, deep, wide),...]
    unnamed x1 -> x3, local copies, waits for them, and re-layouts: 3.15 us -> 4.39 us
where the time goes in v3:
time: 146 us; the launch traced here: 144 us
  Pallas kernels  130 us (89%)
  local copies, waits for them, and re-layouts  9.03 us (6%)
  other arithmetic  4.74 us (3%)
    pallas_call x1, Pallas kernels, gather_multiply(): pl.pallas_call(functools.partial(gather_kernel, plan, early, deep, wide),...  130 us
    unnamed x3, local copies, waits for them, and re-layouts  4.39 us

profile of v3, /device:TPU:25, one launch (start us, length us, event | category | flops | bytes accessed | tf_op | source)
XLA Modules:
  0.0 143.9 jit_solution(429906992477086737)
XLA Ops:
  0.0 2.0 %slice_select_fusion = bf16[280,1280]{1,0:T(8,128)(2,1)} fusion(bf16[280,3360]{1,0:T(8,128)(2,1)} %param.3, pred[1280]{0:T(1024)(128)(4,1)} %constant.4.clone.1), kind=kLoop, calls=%fused_computation.4 | loop fusion | flops 358400 | bytes 1434880 | tf_op jit(solution)/shard_map/jit(_pad)/pad | solution.py:372
  2.0 1.9 %fusion = (bf16[280,1120]{1,0:T(8,128)(2,1)S(1)}, bf16[280,1120]{1,0:T(8,128)(2,1)S(1)}) fusion(bf16[280,3360]{1,0:T(8,128)(2,1)} %param.3), kind=kLoop, calls=%fused_computation.5 | loop fusion | bytes 2508800 | tf_op jit(solution)/shard_map/slice | solution.py:365
  3.9 0.4 copy.3
  4.3 0.6 copy.8
  4.9 0.4 copy.5
  5.3 0.6 copy.9
  6.0 0.3 pad_bitcast_fusion
  6.3 0.1 pad_maximum_fusion.1
  6.4 1.1 copy.7
  7.5 0.5 reshape.18
  8.1 2.6 %pad_maximum_fusion.w_ref = bf16[280,3840]{1,0:T(8,128)(2,1)} fusion(bf16[280,1280]{1,0:T(8,128)(2,1)} %slice_select_fusion, bf16[280,2560]{1,0:T(8,128)(2,1)S(1)} %reshape.18), kind=kLoop, calls=%fused_computation | loop fusion | flops 4300800 | bytes 4300800 | tf_op jit(solution)/shard_map/concatenate | solution.py:372
  10.7 130.0 %gather_multiply.1 = (bf16[960,1120]{1,0:T(8,128)(2,1)}, bf16[2240,3840]{1,0:T(8,128)(2,1)}) custom-call(bf16[960,2240]{1,0:T(8,128)(2,1)} %bitcast.8, bf16[280,3840]{1,0:T(8,128)(2,1)} %pad_maximum_fusion.w_ref), custom_call_target="tpu_custom_call" | custom-call | tf_op jit(solution)/shard_map/gather_multiply/pallas_call | solution.py:318
  140.7 3.1 %copy.11 = bf16[2,6,80,1120]{3,2,1,0:T(8,128)(2,1)} copy(bf16[2,6,80,1120]{3,2,1,0:T(8,128)(2,1)} %bitcast.11) | data formatting | bytes 4300800

commit v4 on v3

--- a/solution.py
+++ b/solution.py
@@ -25,7 +25,7 @@
     return pairs, both, order
 
 
-def gather_kernel(plan, early, deep, wide, x_hbm, w_ref, o_ref, buf, x_vm, w_vm, q_ref,
+def gather_kernel(plan, early, deep, wide, x_hbm, raw_ref, o_ref, buf, x_vm, w_vm, q_ref, w_ref,
                   local, from_core, block_sum, from_y, pair_sum, from_z, to_y, totals, rounded,
                   x_sem, own_sem, load_sem, zs, zr, ys, yr, xs, xr, cs, cr, ss, sr):
     group, t, core = lax.axis_index("groups"), lax.axis_index("tm"), lax.axis_index("space")
@@ -73,6 +73,18 @@
         c = cols(kind, m)
         return pltpu.make_async_copy(w_ref.at[:, c], buf.at[rows(t), c], own_sem.at[slot(kind, m)])
 
+    part = HEADS * HEAD
+    for i in range(2):
+        for h in range(HEADS):
+            first = (i + 1) * part + h * HEAD
+            piece = raw_ref[:, first:min(first + LANES, 3 * part)]
+            if piece.shape[1] < LANES:
+                piece = jnp.concatenate([piece, jnp.zeros((depth, LANES - piece.shape[1]), piece.dtype)], axis=1)
+            w_ref[:, h * step + i * LANES:h * step + (i + 1) * LANES] = piece
+    aligned = part // LANES * LANES
+    w_ref[:, early * step:early * step + aligned] = raw_ref[:, :aligned]
+    w_ref[:, early * step + aligned:] = jnp.concatenate(
+        [raw_ref[:, aligned:part], jnp.zeros((depth, w_ref.shape[1] - early * step - part), w_ref.dtype)], axis=1)
     for tile in everything:
         own_copy(*tile).start()
 
@@ -233,7 +245,7 @@
     def event(when, action):
         events.append((when, len(events), action))
 
-    tile_time, hop = 6.3, 2.5
+    tile_time, hop = 8.0, 3.5
 
     def send_own(tile):
         for dz in range(1, deep):
@@ -276,7 +288,7 @@
     ready, x_end = 0.0, 0.0
     for i, tile in enumerate(order):
         base = i * tile_time
-        event(max(base - 2 * tile_time, -1.0), functools.partial(send_own, tile))
+        event(max(base - 1 * tile_time, -1.0), functools.partial(send_own, tile))
         for dz in range(1, deep):
             event(base + dz * tile_time / (deep - 1), functools.partial(from_z_tile, tile, dz))
         for dz in range(deep):
@@ -308,9 +320,10 @@
 
 def gather_multiply(x, w, deep, wide, early):
     tokens, channels = x.shape
-    depth, columns = w.shape
+    depth = w.shape[0]
     step = 2 * LANES
-    units = columns // step
+    units = early - (-HEADS * HEAD // step)
+    columns = units * step
     plan = unit_plan(units, early)
     split, fetched = len(plan[0]), len(plan[2])
     dma = pltpu.SemaphoreType.DMA
@@ -325,6 +338,7 @@
             pltpu.VMEM((tokens, channels), jnp.bfloat16),
             pltpu.VMEM((units, channels, step), jnp.bfloat16),
             pltpu.VMEM((units - early, tokens, step), jnp.bfloat16),
+            pltpu.VMEM((depth, columns), jnp.bfloat16),
             pltpu.VMEM((HEADS, HEAD, LANES), f32),
             pltpu.VMEM((half, HEAD, LANES), f32),
             pltpu.VMEM((half, HEAD, LANES), f32),
@@ -360,17 +374,9 @@
 def on_device(deep, wide, latents, proj_weight):
     frame_count, band_rows, column_count, channels = latents.shape
     flat = latents.reshape(-1, channels)
-    depth, columns = proj_weight.shape
     part = HEADS * HEAD
-    queries, keys, values = (proj_weight[:, i * part:(i + 1) * part] for i in range(3))
     if wide:
-        gap = ((0, 0), (0, 0), (0, LANES - HEAD))
-        pads = [jnp.pad(a.reshape(depth, HEADS, HEAD), gap) for a in (keys, values)]
-        heads = jnp.stack(pads, axis=2).reshape(depth, 2 * HEADS * LANES)
-        step = 2 * LANES
-        rest = -(-part // step) * step
-        packed = jnp.concatenate([heads, jnp.pad(queries, ((0, 0), (0, rest - part)))], axis=1)
-        attended = gather_multiply(flat, packed, deep, wide, HEADS)
+        attended = gather_multiply(flat, proj_weight, deep, wide, HEADS)
         return attended.reshape(frame_count, band_rows, column_count, part)
     full = lax.all_gather(proj_weight, "tm", axis=0, tiled=True)
     projected = jnp.dot(flat, full, preferred_element_type=jnp.float32).astype(jnp.bfloat16)

time: 146 us -> 134 us (0.918)
  local copies, waits for them, and re-layouts: 9.03 us -> 3.15 us
  other arithmetic: 4.74 us -> 0 us
    slice x3 -> x0, local copies, waits for them, and re-layouts: 2.69 us -> none  [on_device(): proj_weight[:, i * part:(i + 1) * part]]
    concatenate x1 -> x0, other arithmetic: 2.59 us -> none  [on_device(): jnp.concatenate([heads, jnp.pad(queries, ((0, 0), (0, rest - part)))], ax...]
    pad x1 -> x0, other arithmetic: 2.02 us -> none  [on_device(): jnp.pad(queries, ((0, 0), (0, rest - part)))]
    unnamed x3 -> x1, local copies, waits for them, and re-layouts: 4.39 us -> 3.15 us
where the time goes in v4:
time: 134 us; the launch traced here: 132 us
  Pallas kernels  129 us (96%)
  local copies, waits for them, and re-layouts  3.15 us (2%)
    pallas_call x1, Pallas kernels, gather_multiply(): pl.pallas_call(functools.partial(gather_kernel, plan, early, deep, wide),...  129 us
    unnamed x1, local copies, waits for them, and re-layouts  3.15 us

profile of v4, /device:TPU:25, one launch (start us, length us, event | category | flops | bytes accessed | tf_op | source)
XLA Modules:
  0.0 131.8 jit_solution(11932320107077147793)
XLA Ops:
  0.0 128.6 %gather_multiply.1 = (bf16[960,1120]{1,0:T(8,128)(2,1)}, bf16[2240,3840]{1,0:T(8,128)(2,1)}) custom-call(bf16[960,2240]{1,0:T(8,128)(2,1)} %bitcast.2, bf16[280,3360]{1,0:T(8,128)(2,1)} %raw_ref.1), custom_call_target="tpu_custom_call" | custom-call | tf_op jit(solution)/shard_map/gather_multiply/pallas_call | solution.py:331
  128.6 3.1 %copy.4 = bf16[2,6,80,1120]{3,2,1,0:T(8,128)(2,1)} copy(bf16[2,6,80,1120]{3,2,1,0:T(8,128)(2,1)} %bitcast.3) | data formatting | bytes 4300800
